TPU v7x, 256 devices: a whole 4x4x8 slice. The times are simulated.
256 devices in a mesh: day: 8 (over z_hi, core), row: 32 (over z_lo, x, y).
Axes of the slice: x: 4, y: 4, z: 8 (z_hi: 4, z_lo: 2; z = z_hi * 2 + z_lo), core: 2. Of those that a mesh axis runs over, the one named last changes fastest.
Arguments:
- field: float32 [128, 1024, 1024], P('day', 'row'), may hold values from -6 to 6
- basis_day: float32 [128, 128], replicated, as said below
- basis_x: float32 [1024, 1024], replicated, as said below
- basis_y: float32 [1024, 1024], replicated, as said below
- eig_day: float32 [128], replicated, may hold values from 0.05 to 3
- eig_x: float32 [1024], replicated, may hold values from 0.05 to 3
- eig_y: float32 [1024], replicated, may hold values from 0.05 to 3
- noise: float32 [1], replicated, may hold values from 0.1 to 0.5
Outputs:
- weights: float32 [128, 1024, 1024], P('day', 'row')
Inputs may be any that keep to these rules, and one draw needn't show every extreme that they name: basis_day is orthogonal. basis_x is orthogonal. basis_y is orthogonal.
All inputs are finite; a program needn't handle non-finite values.
Results may differ from a plain program's by a relative error of at most 0.00007.
Values sent between devices are 32-bit elements; how exact they have to be, the bound alone decides.
No kernel may reach another device: no remote copies, remote signals or barrier semaphores. Data moves between devices by JAX's collectives and lax.ppermute only.
A program may use at most 128 MiB of HBM per device.

v0:
```python
import functools
import itertools

import jax
import jax.numpy as jnp
from jax import lax
from jax.experimental import pallas as pl
from jax.experimental.pallas import tpu as pltpu
from jax.sharding import Mesh, PartitionSpec as P

F32, BF16 = jnp.float32, jnp.bfloat16
AXES = ("zh", "core", "zl", "x", "y")
ORDER = ("zh", "zl", "core", "x", "y")
NB = 2
ROWS = NB * 256
WIDE = 16


def split(v):
    hi = v.astype(BF16)
    return hi, (v - hi.astype(F32)).astype(BF16)


def dot3(a, b, dims=((1,), (0,))):
    mul = functools.partial(
        lax.dot_general, dimension_numbers=(dims, ((), ())), preferred_element_type=F32
    )
    return mul(a[0], b[0]) + (mul(a[0], b[1]) + mul(a[1], b[0]))


def swap_groups(v):
    group = lax.broadcasted_iota(jnp.int32, v[0].shape, 1) // 32
    low, even = group < 2, group % 2 == 0

    def pair(a, b, keep, left, right):
        return (
            jnp.where(keep, a, pltpu.roll(b, right, 1)),
            jnp.where(keep, pltpu.roll(a, left, 1), b),
        )

    a0, a2 = pair(v[0], v[2], low, 64, 64)
    a1, a3 = pair(v[1], v[3], low, 64, 64)
    w0, w1 = pair(a0, a1, even, 96, 32)
    w2, w3 = pair(a2, a3, even, 96, 32)
    return w0, w1, w2, w3


def forward_y(f_ref, by_ref, out_ref, cols):
    half = pl.program_id(0)
    cols[...] = dot3(split(f_ref[...]), split(by_ref[...])).T
    for bl in range(NB):
        for q in range(4):
            row = half * (4 * NB) + (bl * 4 + q)
            out_ref[pl.ds(row, 256, stride=WIDE), :] = cols[
                pl.ds(bl * 256, 256), pl.ds(q * 128, 128)
            ]


def row_index(shape, dim):
    m = lax.broadcasted_iota(jnp.int32, shape, dim)
    bl = m // 4 % NB
    group, tl, q = m // (16 * NB), m // (4 * NB) % 4, m % 4
    return group * 16 + q * 4 + tl, bl


def day_matrices(basis_day):
    n = 128 * NB
    wide = row_index((n, 128), 0)[0] == lax.broadcasted_iota(jnp.int32, (n, 128), 1)
    tall = row_index((128, n), 1)[0] == lax.broadcasted_iota(jnp.int32, (128, n), 0)
    same = row_index((n, n), 0)[1] == row_index((n, n), 1)[1]
    wide, tall = wide.astype(BF16), tall.astype(BF16)

    def pick(half, dim):
        rows = lax.dot_general(wide, half, (((1,), (dim,)), ((), ())), preferred_element_type=F32)
        both = jnp.dot(rows.astype(BF16), tall, preferred_element_type=F32)
        return jnp.where(same, both, 0.0).astype(BF16)

    halves = split(basis_day)
    return [pick(h, 1) for h in halves], [pick(h, 0) for h in halves]


def middle(mine_ref, noise_ref, eig_y_ref, r_ref, bx_ref, bd_ref, ed_ref, ex_ref, out_ref, work):
    bx = split(bx_ref[...])
    to_s, to_t = day_matrices(bd_ref[...])
    day, bl = row_index((128 * NB, 128), 0)
    chosen = day == lax.broadcasted_iota(jnp.int32, day.shape, 1)
    ed = jnp.sum(jnp.where(chosen, ed_ref[...], 0.0), 1, keepdims=True)
    edx = ed * ex_ref[...]
    w = 4 * NB

    def blocks(half):
        for zh, zl, core, x in itertools.product(range(4), range(2), range(2), range(4)):
            device = ((zh * 2 + zl) * 2 + core) * 16 + x * 4
            ys = [pl.ds((device + y) * WIDE + half * w, w) for y in range(4)]
            tls = [pl.ds(((zh * 2 + core) * 4 + tl) * w, w) for tl in range(4)]
            yield ys, tls, pl.ds((zl * 4 + x) * 128, 128)

    for half in range(WIDE // w):
        first = half * ROWS
        for ys, tls, lanes in blocks(half):
            for rows, part in zip(tls, swap_groups([r_ref[y, :] for y in ys])):
                work[rows, lanes] = part
        ey = jnp.full(ed.shape, eig_y_ref[first + mine_ref[0]], F32)
        for i in range(1, NB):
            ey = jnp.where(bl[:, :1] == i, eig_y_ref[first + i * 256 + mine_ref[0]], ey)
        along_x = dot3(split(work[...]), bx)
        spectral = dot3(to_s, split(along_x))
        back_day = dot3(to_t, split(spectral / (edx * ey + noise_ref[0])))
        work[...] = dot3(split(back_day), bx, ((1,), (1,)))
        for ys, tls, lanes in blocks(half):
            for rows, part in zip(ys, swap_groups([work[t, lanes] for t in tls])):
                out_ref[rows, :] = part


def inverse_y(r_ref, by_ref, out_ref, cols):
    for bl in range(WIDE // 4):
        for q in range(4):
            cols[pl.ds(bl * 256, 256), pl.ds(q * 128, 128)] = r_ref[
                pl.ds(bl * 4 + q, 256, stride=WIDE), :
            ]
    out_ref[...] = dot3(split(cols[...].T), split(by_ref[...]), ((1,), (1,)))


VMEM = pl.BlockSpec(memory_space=pltpu.VMEM)
SMEM = pl.BlockSpec(memory_space=pltpu.SMEM)
PARAMS = pltpu.CompilerParams(vmem_limit_bytes=40 << 20)


def exchange(flat):
    parts = flat.reshape(256, WIDE, 128)
    return lax.all_to_all(parts, ORDER, 0, 0, tiled=True).reshape(flat.shape)


def body(field, basis_day, basis_x, basis_y, eig_day, eig_x, eig_y, noise):
    days, rows, cols = field.shape
    mine = lax.axis_index(ORDER).astype(jnp.int32).reshape(1)
    flat = field.reshape(days * rows, cols)
    wire = jax.ShapeDtypeStruct((256 * WIDE, 128), F32)
    sent = pl.pallas_call(
        forward_y,
        out_shape=wire,
        grid=(cols // ROWS,),
        in_specs=[
            pl.BlockSpec(flat.shape, lambda c: (0, 0)),
            pl.BlockSpec((cols, ROWS), lambda c: (0, c)),
        ],
        out_specs=pl.BlockSpec(wire.shape, lambda c: (0, 0)),
        scratch_shapes=[pltpu.VMEM((ROWS, days * rows), F32)],
        compiler_params=PARAMS,
        name="forward_y",
    )(flat, basis_y)
    solved = pl.pallas_call(
        middle,
        out_shape=wire,
        in_specs=[SMEM] * 3 + [VMEM] * 5,
        out_specs=VMEM,
        scratch_shapes=[pltpu.VMEM((128 * NB, cols), F32)],
        compiler_params=PARAMS,
        name="middle",
    )(mine, noise, eig_y, exchange(sent), basis_x, basis_day, eig_day.reshape(1, -1), eig_x.reshape(1, -1))
    weights = pl.pallas_call(
        inverse_y,
        out_shape=jax.ShapeDtypeStruct(flat.shape, F32),
        in_specs=[VMEM] * 2,
        out_specs=VMEM,
        scratch_shapes=[pltpu.VMEM((cols, days * rows), F32)],
        compiler_params=PARAMS,
        name="inverse_y",
    )(exchange(solved), basis_y)
    return weights.reshape(days, rows, cols)


def solution(mesh):
    fine = Mesh(mesh.devices.reshape(4, 2, 2, 4, 4), AXES)
    spec = P(("zh", "core"), ("zl", "x", "y"), None)
    in_specs = (spec, P(), P(), P(), P(), P(), P(), P())
    return jax.shard_map(body, mesh=fine, in_specs=in_specs, out_specs=spec, check_vma=False)
```

profile of v0, /device:TPU:1, one launch (start us, length us, event | category | flops | bytes accessed | tf_op | source)
XLA Modules:
  0.0 155.0 jit_solution(11355044418710538154)
XLA Ops:
  0.0 0.0 copy-start
  0.0 2.2 %copy-done = f32[1024,1024]{1,0:T(8,128)S(1)} copy-done((f32[1024,1024]{1,0:T(8,128)S(1)}, f32[1024,1024]{1,0:T(8,128)}, u32[]{:S(2)}) %copy-start) | copy-done | bytes 4194328
  2.2 0.0 copy-start.4
  2.2 1.6 %copy-done.4 = f32[16,32,1024]{2,1,0:T(8,128)S(1)} copy-done((f32[16,32,1024]{2,1,0:T(8,128)S(1)}, f32[16,32,1024]{2,1,0:T(8,128)}, u32[]{:S(2)}) %copy-start.4) | copy-done | bytes 2097176
  3.8 4.9 %forward_y.1 = f32[4096,128]{1,0:T(8,128)S(1)} custom-call(f32[512,1024]{1,0:T(8,128)S(1)} %bitcast.13, f32[1024,1024]{1,0:T(8,128)S(1)} %copy-done), custom_call_target="tpu_custom_call" | custom-call | tf_op jit(solution)/shard_map/forward_y/pallas_call | solution.py:139
  8.7 0.0 copy-start.2
  8.7 1.3 copy-done.2
  10.0 0.0 copy-start.5
  10.0 0.0 copy-start.6
  10.0 0.0 copy-start.7
  10.0 0.0 copy-start.8
  10.0 15.7 %all-to-all-start = ((f32[256,16,128]{2,1,0:T(8,128)}), f32[256,16,128]{2,1,0:T(8,128)S(1)}, u32[]{:S(2)}, u32[]{:S(2)}) async-start(f32[256,16,128]{2,1,0:T(8,128)} %bitcast.10), calls=%async_computation | async-start | bytes 4194304 | tf_op jit(solution)/shard_map/all_to_all | solution.py:131
  26.3 51.6 %all-to-all-done = f32[256,16,128]{2,1,0:T(8,128)S(1)} async-done(((f32[256,16,128]{2,1,0:T(8,128)}), f32[256,16,128]{2,1,0:T(8,128)S(1)}, u32[]{:S(2)}, u32[]{:S(2)}) %all-to-all-start) | async-done | bytes 2097184 | tf_op jit(solution)/shard_map/all_to_all | solution.py:131
  77.9 0.0 copy-done.5
  77.9 0.0 copy-done.6
  77.9 0.0 copy-done.7
  77.9 0.0 copy-done.8
  77.9 0.0 copy-start.3
  77.9 2.2 %copy-done.3 = f32[1024,1024]{1,0:T(8,128)S(1)} copy-done((f32[1024,1024]{1,0:T(8,128)S(1)}, f32[1024,1024]{1,0:T(8,128)}, u32[]{:S(2)}) %copy-start.3) | copy-done | bytes 4194328
  80.1 9.9 %middle.1 = f32[4096,128]{1,0:T(8,128)S(1)} custom-call(s32[1]{0:T(128)} %bitcast.mine_ref, f32[1]{0:T(128)S(6)} %copy.9.noise_ref, f32[1024]{0:T(1024)S(1)} %copy-done.6, f32[4096,128]{1,0:T(8,128)S(1)} %bitcast.9, f32[1024,1024]{1,0:T(8,128)S(1)} %copy-done.3, f32[128,128]{1,0:T(8,128)S(1)} %copy-done.5, f32[1,128]{1,0:T(1,128)S(1)} %bitcast.15, ...), custom_call_target="tpu_custom_call" | custom-call | tf_op jit(solution)/shard_map/middle/pallas_call | solution.py:152
  90.0 0.0 copy-start.1
  90.0 59.6 %all_to_all.10 = f32[256,16,128]{2,1,0:T(8,128)S(1)} all-to-all(f32[256,16,128]{2,1,0:T(8,128)S(1)} %bitcast.11), channel_id=1, replica_groups=mesh['zh'=4,'core'=2,'zl'=2,'x'=4,'y'=4] {'zh','zl','core','x','y'}, dimensions={0} | all-to-all | bytes 4194304 | tf_op jit(solution)/shard_map/all_to_all | solution.py:131
  149.6 0.0 copy-done.1
  149.6 5.4 %inverse_y.1 = f32[512,1024]{1,0:T(8,128)} custom-call(f32[4096,128]{1,0:T(8,128)S(1)} %bitcast.12, f32[1024,1024]{1,0:T(8,128)S(1)} %copy-done.1), custom_call_target="tpu_custom_call" | custom-call | tf_op jit(solution)/shard_map/inverse_y/pallas_call | solution.py:161
Async XLA Ops:
  0.0 2.2 %copy-start = (f32[1024,1024]{1,0:T(8,128)S(1)}, f32[1024,1024]{1,0:T(8,128)}, u32[]{:S(2)}) copy-start(f32[1024,1024]{1,0:T(8,128)} %by_ref.3) | copy-start | bytes 12582916
  2.2 1.6 %copy-start.4 = (f32[16,32,1024]{2,1,0:T(8,128)S(1)}, f32[16,32,1024]{2,1,0:T(8,128)}, u32[]{:S(2)}) copy-start(f32[16,32,1024]{2,1,0:T(8,128)} %param.8) | copy-start | bytes 6291460
  8.7 1.3 copy-start.2
  10.0 67.9 %copy-start.5 = (f32[128,128]{1,0:T(8,128)S(1)}, f32[128,128]{1,0:T(8,128)}, u32[]{:S(2)}) copy-start(f32[128,128]{1,0:T(8,128)} %bd_ref.1) | copy-start | bytes 196612
  10.0 67.9 %copy-start.6 = (f32[1024]{0:T(1024)S(1)}, f32[1024]{0:T(1024)}, u32[]{:S(2)}) copy-start(f32[1024]{0:T(1024)} %eig_y_ref.1) | copy-start | bytes 12292
  10.0 67.9 %copy-start.7 = (f32[1024]{0:T(1024)S(1)}, f32[1024]{0:T(1024)}, u32[]{:S(2)}) copy-start(f32[1024]{0:T(1024)} %param.13) | copy-start | bytes 12292
  10.0 67.9 %copy-start.8 = (f32[128]{0:T(128)S(1)}, f32[128]{0:T(128)}, u32[]{:S(2)}) copy-start(f32[128]{0:T(128)} %param.12) | copy-start | bytes 1540
  10.0 67.9 %all-to-all-start = ((f32[256,16,128]{2,1,0:T(8,128)}), f32[256,16,128]{2,1,0:T(8,128)S(1)}, u32[]{:S(2)}, u32[]{:S(2)}) async-start(f32[256,16,128]{2,1,0:T(8,128)} %bitcast.10), calls=%async_computation | async-start | bytes 4194304 | tf_op jit(solution)/shard_map/all_to_all | solution.py:131
  77.9 2.2 %copy-start.3 = (f32[1024,1024]{1,0:T(8,128)S(1)}, f32[1024,1024]{1,0:T(8,128)}, u32[]{:S(2)}) copy-start(f32[1024,1024]{1,0:T(8,128)} %bx_ref.1) | copy-start | bytes 12582916
  90.0 59.6 %copy-start.1 = (f32[1024,1024]{1,0:T(8,128)S(1)}, f32[1024,1024]{1,0:T(8,128)}, u32[]{:S(2)}) copy-start(f32[1024,1024]{1,0:T(8,128)} %by_ref.3) | copy-start | bytes 12582916
where the time goes:
time: 155 us
  blocking collectives  59.6 us (38%)
  waiting for transfers between devices  51.6 us (33%)
  Pallas kernels  20.2 us (13%)
  starting transfers between devices  15.7 us (10%)
  local copies, waits for them, and re-layouts  7.3 us (5%)
    all_to_all x1, blocking collectives, exchange(): return lax.all_to_all(parts, ORDER, 0, 0, tiled=True).reshape(flat.shape)  59.6 us
    all_to_all x1, waiting for transfers between devices, exchange(): return lax.all_to_all(parts, ORDER, 0, 0, tiled=True).reshape(flat.shape)  51.6 us
    all_to_all x1, starting transfers between devices, exchange(): return lax.all_to_all(parts, ORDER, 0, 0, tiled=True).reshape(flat.shape)  15.7 us
    pallas_call x1, Pallas kernels, body(): pl.pallas_call(middle, out_shape=wire, in_specs=[SMEM] * 3 + [VMEM] * 5,...  9.86 us
    unnamed x18, local copies, waits for them, and re-layouts  7.3 us
    pallas_call x1, Pallas kernels, body(): pl.pallas_call(inverse_y, out_shape=jax.ShapeDtypeStruct(flat.shape, F32)...  5.43 us
    pallas_call x1, Pallas kernels, body(): pl.pallas_call(forward_y, out_shape=wire, grid=(cols // ROWS,), in_specs=...  4.88 us
  transfers between devices with their start and end apart: 1, of which 1 were waited for; matrix products, arithmetic and copies ran while one was open for 0% of the time, Pallas kernels for 0%

commit v1 on v0

--- a/solution.py
+++ b/solution.py
@@ -45,13 +45,13 @@
     return w0, w1, w2, w3
 
 
-def forward_y(f_ref, by_ref, out_ref, cols):
-    half = pl.program_id(0)
-    cols[...] = dot3(split(f_ref[...]), split(by_ref[...])).T
+def forward_y(noise_ref, f_ref, by_ref, out_ref, level_ref, cols):
+    level_ref[...] = jnp.full(level_ref.shape, noise_ref[0], F32)
+    cols[...] = dot3(split(by_ref[...]), split(f_ref[...]), ((0,), (1,)))
+    out = out_ref.reshape(256 * 4 * NB, 128)
     for bl in range(NB):
         for q in range(4):
-            row = half * (4 * NB) + (bl * 4 + q)
-            out_ref[pl.ds(row, 256, stride=WIDE), :] = cols[
+            out[pl.ds(bl * 4 + q, 256, stride=4 * NB), :] = cols[
                 pl.ds(bl * 256, 256), pl.ds(q * 128, 128)
             ]
 
@@ -79,7 +79,7 @@
     return [pick(h, 1) for h in halves], [pick(h, 0) for h in halves]
 
 
-def middle(mine_ref, noise_ref, eig_y_ref, r_ref, bx_ref, bd_ref, ed_ref, ex_ref, out_ref, work):
+def middle(r_ref, bx_ref, bd_ref, ed_ref, ex_ref, ey_ref, noise_ref, out_ref, work):
     bx = split(bx_ref[...])
     to_s, to_t = day_matrices(bd_ref[...])
     day, bl = row_index((128 * NB, 128), 0)
@@ -87,6 +87,8 @@
     ed = jnp.sum(jnp.where(chosen, ed_ref[...], 0.0), 1, keepdims=True)
     edx = ed * ex_ref[...]
     w = 4 * NB
+    column = lax.broadcasted_iota(jnp.int32, ey_ref.shape, 1)
+    mine = lax.axis_index(ORDER)
 
     def blocks(half):
         for zh, zl, core, x in itertools.product(range(4), range(2), range(2), range(4)):
@@ -96,75 +98,99 @@
             yield ys, tls, pl.ds((zl * 4 + x) * 128, 128)
 
     for half in range(WIDE // w):
-        first = half * ROWS
         for ys, tls, lanes in blocks(half):
             for rows, part in zip(tls, swap_groups([r_ref[y, :] for y in ys])):
                 work[rows, lanes] = part
-        ey = jnp.full(ed.shape, eig_y_ref[first + mine_ref[0]], F32)
-        for i in range(1, NB):
-            ey = jnp.where(bl[:, :1] == i, eig_y_ref[first + i * 256 + mine_ref[0]], ey)
+        ey = jnp.zeros_like(ed)
+        for i in range(NB):
+            own = jnp.where(column == half * ROWS + i * 256 + mine, ey_ref[...], 0.0)
+            ey = jnp.where(bl[:, :1] == i, jnp.sum(own, 1, keepdims=True), ey)
         along_x = dot3(split(work[...]), bx)
         spectral = dot3(to_s, split(along_x))
-        back_day = dot3(to_t, split(spectral / (edx * ey + noise_ref[0])))
+        back_day = dot3(to_t, split(spectral / (edx * ey + noise_ref[:1, :1])))
         work[...] = dot3(split(back_day), bx, ((1,), (1,)))
         for ys, tls, lanes in blocks(half):
             for rows, part in zip(ys, swap_groups([work[t, lanes] for t in tls])):
                 out_ref[rows, :] = part
 
 
-def inverse_y(r_ref, by_ref, out_ref, cols):
-    for bl in range(WIDE // 4):
-        for q in range(4):
-            cols[pl.ds(bl * 256, 256), pl.ds(q * 128, 128)] = r_ref[
-                pl.ds(bl * 4 + q, 256, stride=WIDE), :
-            ]
-    out_ref[...] = dot3(split(cols[...].T), split(by_ref[...]), ((1,), (1,)))
+def inverse_y(r_ref, by_ref, out_ref, cols, high, low):
+    @pl.when(pl.program_id(0) == 0)
+    def _():
+        for bl in range(WIDE // 4):
+            for q in range(4):
+                cols[pl.ds(bl * 256, 256), pl.ds(q * 128, 128)] = r_ref[
+                    pl.ds(bl * 4 + q, 256, stride=WIDE), :
+                ]
+        high[...], low[...] = split(cols[...].T)
+
+    out_ref[...] = dot3((high[...], low[...]), split(by_ref[...]), ((1,), (1,)))
 
 
 VMEM = pl.BlockSpec(memory_space=pltpu.VMEM)
-SMEM = pl.BlockSpec(memory_space=pltpu.SMEM)
-PARAMS = pltpu.CompilerParams(vmem_limit_bytes=40 << 20)
-
-
-def exchange(flat):
-    parts = flat.reshape(256, WIDE, 128)
-    return lax.all_to_all(parts, ORDER, 0, 0, tiled=True).reshape(flat.shape)
+
+
+def limit(mib):
+    return pltpu.CompilerParams(vmem_limit_bytes=mib << 20)
+
+
+def exchange(parts):
+    parts = parts.reshape(256, WIDE, 128)
+    return lax.all_to_all(parts, ORDER, 0, 0, tiled=True).reshape(256 * WIDE, 128)
 
 
 def body(field, basis_day, basis_x, basis_y, eig_day, eig_x, eig_y, noise):
     days, rows, cols = field.shape
-    mine = lax.axis_index(ORDER).astype(jnp.int32).reshape(1)
     flat = field.reshape(days * rows, cols)
-    wire = jax.ShapeDtypeStruct((256 * WIDE, 128), F32)
-    sent = pl.pallas_call(
+    sent, level = pl.pallas_call(
         forward_y,
-        out_shape=wire,
+        out_shape=[jax.ShapeDtypeStruct((256, WIDE, 128), F32), jax.ShapeDtypeStruct((8, 128), F32)],
         grid=(cols // ROWS,),
         in_specs=[
+            pl.BlockSpec(memory_space=pltpu.SMEM),
             pl.BlockSpec(flat.shape, lambda c: (0, 0)),
             pl.BlockSpec((cols, ROWS), lambda c: (0, c)),
         ],
-        out_specs=pl.BlockSpec(wire.shape, lambda c: (0, 0)),
+        out_specs=[
+            pl.BlockSpec((256, 4 * NB, 128), lambda c: (0, c, 0)),
+            pl.BlockSpec((8, 128), lambda c: (0, 0)),
+        ],
         scratch_shapes=[pltpu.VMEM((ROWS, days * rows), F32)],
-        compiler_params=PARAMS,
+        compiler_params=limit(60),
         name="forward_y",
-    )(flat, basis_y)
+    )(noise, flat, basis_y)
     solved = pl.pallas_call(
         middle,
-        out_shape=wire,
-        in_specs=[SMEM] * 3 + [VMEM] * 5,
+        out_shape=jax.ShapeDtypeStruct((256 * WIDE, 128), F32),
+        in_specs=[VMEM] * 7,
         out_specs=VMEM,
         scratch_shapes=[pltpu.VMEM((128 * NB, cols), F32)],
-        compiler_params=PARAMS,
+        compiler_params=limit(32),
         name="middle",
-    )(mine, noise, eig_y, exchange(sent), basis_x, basis_day, eig_day.reshape(1, -1), eig_x.reshape(1, -1))
+    )(
+        exchange(sent),
+        basis_x,
+        basis_day,
+        eig_day.reshape(1, -1),
+        eig_x.reshape(1, -1),
+        eig_y.reshape(1, -1),
+        level,
+    )
     weights = pl.pallas_call(
         inverse_y,
         out_shape=jax.ShapeDtypeStruct(flat.shape, F32),
-        in_specs=[VMEM] * 2,
-        out_specs=VMEM,
-        scratch_shapes=[pltpu.VMEM((cols, days * rows), F32)],
-        compiler_params=PARAMS,
+        grid=(2,),
+        in_specs=[
+            pl.BlockSpec((256 * WIDE, 128), lambda c: (0, 0)),
+            pl.BlockSpec((cols // 2, cols), lambda c: (c, 0)),
+        ],
+        out_specs=pl.BlockSpec((days * rows, cols // 2), lambda c: (0, c)),
+        scratch_shapes=[
+            pltpu.VMEM((cols, days * rows), F32),
+            pltpu.VMEM((days * rows, cols), BF16),
+            pltpu.VMEM((days * rows, cols), BF16),
+        ],
+        compiler_params=limit(40),
         name="inverse_y",
     )(exchange(solved), basis_y)
     return weights.reshape(days, rows, cols)

time: 155 us -> 151 us (0.974)
  blocking collectives: 59.6 us -> 127 us
  waiting for transfers between devices: 51.6 us -> 0 us
  starting transfers between devices: 15.7 us -> 0 us
  local copies, waits for them, and re-layouts: 7.3 us -> 0.69 us
  Pallas kernels: 20.2 us -> 21.9 us
    all_to_all x1 -> x2, blocking collectives: 59.6 us -> 127 us  [exchange(): lax.all_to_all(parts, ORDER, 0, 0, tiled=True).reshape(256 * WIDE, 128)]
    all_to_all x1 -> x0, waiting for transfers between devices: 51.6 us -> none  [exchange(): return lax.all_to_all(parts, ORDER, 0, 0, tiled=True).reshape(flat.shape)]
    all_to_all x1 -> x0, starting transfers between devices: 15.7 us -> none  [exchange(): return lax.all_to_all(parts, ORDER, 0, 0, tiled=True).reshape(flat.shape)]
    unnamed x18 -> x14, local copies, waits for them, and re-layouts: 7.3 us -> 0.69 us
    pallas_call x2, Pallas kernels: 14.7 us -> 16.6 us  [the longest x1 9.48 us: body(): pl.pallas_call(middle, out_shape=jax.ShapeDtypeStruct((256 * WIDE, 128),...]
  transfers between devices with their start and end apart: 1 -> 0, of which waited for: 1 -> 0; matrix products, arithmetic and copies ran while one was open for 0% -> 0% of each run, Pallas kernels for 0% -> 0%
where the time goes in v1:
time: 151 us
  blocking collectives  127 us (84%)
  Pallas kernels  21.9 us (15%)
    all_to_all x2, blocking collectives, exchange(): lax.all_to_all(parts, ORDER, 0, 0, tiled=True).reshape(256 * WIDE, 128)  127 us
    pallas_call x1, Pallas kernels, body(): pl.pallas_call(middle, out_shape=jax.ShapeDtypeStruct((256 * WIDE, 128),...  9.48 us
    pallas_call x1, Pallas kernels, body(): pl.pallas_call(forward_y, out_shape=[jax.ShapeDtypeStruct((256, WIDE, 128...  7.08 us
    pallas_call x1, Pallas kernels, body(): pl.pallas_call(inverse_y, out_shape=jax.ShapeDtypeStruct(flat.shape, F32)...  5.39 us

profile of v1, /device:TPU:1, one launch (start us, length us, event | category | flops | bytes accessed | tf_op | source)
XLA Modules:
  0.0 150.8 jit_solution(6985203035802425644)
XLA Ops:
  0.7 0.0 copy-start.2
  0.7 7.1 %forward_y.1 = (f32[256,16,128]{2,1,0:T(8,128)}, f32[8,128]{1,0:T(8,128)}) custom-call(f32[1]{0:T(128)S(6)} %copy.9.noise_ref, f32[512,1024]{1,0:T(8,128)} %bitcast.14, f32[1024,1024]{1,0:T(8,128)} %by_ref.3), custom_call_target="tpu_custom_call" | custom-call | tf_op jit(solution)/shard_map/forward_y/pallas_call | solution.py:145
  7.7 0.0 copy-start.1
  7.7 0.0 copy-start.3
  7.7 0.0 copy-start.4
  7.7 0.0 copy-start.6
  7.8 67.9 %all_to_all.10 = f32[256,16,128]{2,1,0:T(8,128)S(1)} all-to-all(f32[256,16,128]{2,1,0:T(8,128)} %get-tuple-element.7), channel_id=1, replica_groups=mesh['zh'=4,'core'=2,'zl'=2,'x'=4,'y'=4] {'zh','zl','core','x','y'}, dimensions={0} | all-to-all | bytes 4194304 | tf_op jit(solution)/shard_map/all_to_all | solution.py:139
  75.7 0.0 copy-done.2
  75.7 0.0 copy-done.1
  75.7 0.0 copy-done.3
  75.7 0.0 copy-done.4
  75.7 0.0 copy-done.6
  75.7 0.0 copy-start.5
  75.7 0.7 copy-done.5
  76.4 9.5 %middle.1 = f32[4096,128]{1,0:T(8,128)S(1)} custom-call(f32[4096,128]{1,0:T(8,128)S(1)} %bitcast.8, f32[1024,1024]{1,0:T(8,128)S(1)} %copy-done.1, f32[128,128]{1,0:T(8,128)S(1)} %copy-done.2, f32[1,128]{1,0:T(1,128)S(1)} %bitcast.13, f32[1,1024]{1,0:T(1,128)S(1)} %bitcast.11, f32[1,1024]{1,0:T(1,128)S(1)} %bitcast.12, f32[8,128]{1,0:T(8,128)S(1)} %copy-done.5), custom_call_target="tpu_custom_call" | custom-call | tf_op jit(solution)/shard_map/middle/pallas_call | solution.py:162
  85.8 0.0 copy-start
  85.9 59.6 %all_to_all.11 = f32[256,16,128]{2,1,0:T(8,128)S(1)} all-to-all(f32[256,16,128]{2,1,0:T(8,128)S(1)} %bitcast.9), channel_id=1, replica_groups=mesh['zh'=4,'core'=2,'zl'=2,'x'=4,'y'=4] {'zh','zl','core','x','y'}, dimensions={0} | all-to-all | bytes 4194304 | tf_op jit(solution)/shard_map/all_to_all | solution.py:139
  145.4 0.0 copy-done
  145.4 5.4 %inverse_y.1 = f32[512,1024]{1,0:T(8,128)} custom-call(f32[4096,128]{1,0:T(8,128)S(1)} %bitcast.10, f32[1024,1024]{1,0:T(8,128)S(1)} %copy-done), custom_call_target="tpu_custom_call" | custom-call | tf_op jit(solution)/shard_map/inverse_y/pallas_call | solution.py:179
Async XLA Ops:
  0.7 75.0 %copy-start.2 = (f32[128,128]{1,0:T(8,128)S(1)}, f32[128,128]{1,0:T(8,128)}, u32[]{:S(2)}) copy-start(f32[128,128]{1,0:T(8,128)} %bd_ref.1) | copy-start | bytes 196612
  7.7 67.9 %copy-start.1 = (f32[1024,1024]{1,0:T(8,128)S(1)}, f32[1024,1024]{1,0:T(8,128)}, u32[]{:S(2)}) copy-start(f32[1024,1024]{1,0:T(8,128)} %bx_ref.1) | copy-start | bytes 12582916
  7.7 67.9 %copy-start.3 = (f32[1024]{0:T(1024)S(1)}, f32[1024]{0:T(1024)}, u32[]{:S(2)}) copy-start(f32[1024]{0:T(1024)} %param.13) | copy-start | bytes 12292
  7.7 67.9 %copy-start.4 = (f32[1024]{0:T(1024)S(1)}, f32[1024]{0:T(1024)}, u32[]{:S(2)}) copy-start(f32[1024]{0:T(1024)} %param.14) | copy-start | bytes 12292
  7.7 67.9 %copy-start.6 = (f32[128]{0:T(128)S(1)}, f32[128]{0:T(128)}, u32[]{:S(2)}) copy-start(f32[128]{0:T(128)} %param.12) | copy-start | bytes 1540
  75.7 0.7 copy-start.5
  85.8 59.6 %copy-start = (f32[1024,1024]{1,0:T(8,128)S(1)}, f32[1024,1024]{1,0:T(8,128)}, u32[]{:S(2)}) copy-start(f32[1024,1024]{1,0:T(8,128)} %by_ref.3) | copy-start | bytes 12582916

commit v2 on v1

--- a/solution.py
+++ b/solution.py
@@ -45,8 +45,7 @@
     return w0, w1, w2, w3
 
 
-def forward_y(noise_ref, f_ref, by_ref, out_ref, level_ref, cols):
-    level_ref[...] = jnp.full(level_ref.shape, noise_ref[0], F32)
+def forward_y(_, f_ref, by_ref, out_ref, cols):
     cols[...] = dot3(split(by_ref[...]), split(f_ref[...]), ((0,), (1,)))
     out = out_ref.reshape(256 * 4 * NB, 128)
     for bl in range(NB):
@@ -107,7 +106,7 @@
             ey = jnp.where(bl[:, :1] == i, jnp.sum(own, 1, keepdims=True), ey)
         along_x = dot3(split(work[...]), bx)
         spectral = dot3(to_s, split(along_x))
-        back_day = dot3(to_t, split(spectral / (edx * ey + noise_ref[:1, :1])))
+        back_day = dot3(to_t, split(spectral / (edx * ey + noise_ref[0])))
         work[...] = dot3(split(back_day), bx, ((1,), (1,)))
         for ys, tls, lanes in blocks(half):
             for rows, part in zip(ys, swap_groups([work[t, lanes] for t in tls])):
@@ -142,19 +141,16 @@
 def body(field, basis_day, basis_x, basis_y, eig_day, eig_x, eig_y, noise):
     days, rows, cols = field.shape
     flat = field.reshape(days * rows, cols)
-    sent, level = pl.pallas_call(
+    sent = pl.pallas_call(
         forward_y,
-        out_shape=[jax.ShapeDtypeStruct((256, WIDE, 128), F32), jax.ShapeDtypeStruct((8, 128), F32)],
+        out_shape=jax.ShapeDtypeStruct((256, WIDE, 128), F32),
         grid=(cols // ROWS,),
         in_specs=[
             pl.BlockSpec(memory_space=pltpu.SMEM),
             pl.BlockSpec(flat.shape, lambda c: (0, 0)),
             pl.BlockSpec((cols, ROWS), lambda c: (0, c)),
         ],
-        out_specs=[
-            pl.BlockSpec((256, 4 * NB, 128), lambda c: (0, c, 0)),
-            pl.BlockSpec((8, 128), lambda c: (0, 0)),
-        ],
+        out_specs=pl.BlockSpec((256, 4 * NB, 128), lambda c: (0, c, 0)),
         scratch_shapes=[pltpu.VMEM((ROWS, days * rows), F32)],
         compiler_params=limit(60),
         name="forward_y",
@@ -162,7 +158,7 @@
     solved = pl.pallas_call(
         middle,
         out_shape=jax.ShapeDtypeStruct((256 * WIDE, 128), F32),
-        in_specs=[VMEM] * 7,
+        in_specs=[VMEM] * 6 + [pl.BlockSpec(memory_space=pltpu.SMEM)],
         out_specs=VMEM,
         scratch_shapes=[pltpu.VMEM((128 * NB, cols), F32)],
         compiler_params=limit(32),
@@ -174,7 +170,7 @@
         eig_day.reshape(1, -1),
         eig_x.reshape(1, -1),
         eig_y.reshape(1, -1),
-        level,
+        noise,
     )
     weights = pl.pallas_call(
         inverse_y,

time: 151 us -> 150 us (level)
  no operation moved by 1% of the time
where the time goes in v2:
time: 150 us
  blocking collectives  127 us (85%)
  Pallas kernels  21.7 us (14%)
    all_to_all x2, blocking collectives, exchange(): lax.all_to_all(parts, ORDER, 0, 0, tiled=True).reshape(256 * WIDE, 128)  127 us
    pallas_call x1, Pallas kernels, body(): pl.pallas_call(middle, out_shape=jax.ShapeDtypeStruct((256 * WIDE, 128),...  9.27 us
    pallas_call x1, Pallas kernels, body(): pl.pallas_call(forward_y, out_shape=jax.ShapeDtypeStruct((256, WIDE, 128)...  7.05 us
    pallas_call x1, Pallas kernels, body(): pl.pallas_call(inverse_y, out_shape=jax.ShapeDtypeStruct(flat.shape, F32)...  5.39 us

profile of v2, /device:TPU:1, one launch (start us, length us, event | category | flops | bytes accessed | tf_op | source)
XLA Modules:
  0.0 149.9 jit_solution(10855681953633468303)
XLA Ops:
  0.7 0.0 copy-start.2
  0.7 0.0 copy-start.4
  0.7 7.1 %forward_y.1 = f32[256,16,128]{2,1,0:T(8,128)} custom-call(f32[1]{0:T(128)S(6)} %copy.9._.noise_ref, f32[512,1024]{1,0:T(8,128)} %bitcast.14, f32[1024,1024]{1,0:T(8,128)} %by_ref.3), custom_call_target="tpu_custom_call" | custom-call | tf_op jit(solution)/shard_map/forward_y/pallas_call | solution.py:144
  7.7 0.0 copy-start.1
  7.7 0.0 copy-start.3
  7.7 0.0 copy-start.5
  7.7 67.9 %all_to_all.10 = f32[256,16,128]{2,1,0:T(8,128)S(1)} all-to-all(f32[256,16,128]{2,1,0:T(8,128)} %forward_y.1), channel_id=1, replica_groups=mesh['zh'=4,'core'=2,'zl'=2,'x'=4,'y'=4] {'zh','zl','core','x','y'}, dimensions={0} | all-to-all | bytes 4194304 | tf_op jit(solution)/shard_map/all_to_all | solution.py:138
  75.6 0.0 copy-done.2
  75.6 0.0 copy-done.4
  75.6 0.0 copy-done.1
  75.6 0.0 copy-done.3
  75.7 0.0 copy-done.5
  75.7 9.3 %middle.1 = f32[4096,128]{1,0:T(8,128)S(1)} custom-call(f32[4096,128]{1,0:T(8,128)S(1)} %bitcast.8, f32[1024,1024]{1,0:T(8,128)S(1)} %copy-done.1, f32[128,128]{1,0:T(8,128)S(1)} %copy-done.2, f32[1,128]{1,0:T(1,128)S(1)} %bitcast.13, f32[1,1024]{1,0:T(1,128)S(1)} %bitcast.11, f32[1,1024]{1,0:T(1,128)S(1)} %bitcast.12, f32[1]{0:T(128)S(6)} %copy.9._.noise_ref), custom_call_target="tpu_custom_call" | custom-call | tf_op jit(solution)/shard_map/middle/pallas_call | solution.py:158
  84.9 0.0 copy-start
  85.0 59.6 %all_to_all.11 = f32[256,16,128]{2,1,0:T(8,128)S(1)} all-to-all(f32[256,16,128]{2,1,0:T(8,128)S(1)} %bitcast.9), channel_id=1, replica_groups=mesh['zh'=4,'core'=2,'zl'=2,'x'=4,'y'=4] {'zh','zl','core','x','y'}, dimensions={0} | all-to-all | bytes 4194304 | tf_op jit(solution)/shard_map/all_to_all | solution.py:138
  144.5 0.0 copy-done
  144.5 5.4 %inverse_y.1 = f32[512,1024]{1,0:T(8,128)} custom-call(f32[4096,128]{1,0:T(8,128)S(1)} %bitcast.10, f32[1024,1024]{1,0:T(8,128)S(1)} %copy-done), custom_call_target="tpu_custom_call" | custom-call | tf_op jit(solution)/shard_map/inverse_y/pallas_call | solution.py:175
Async XLA Ops:
  0.7 75.0 %copy-start.2 = (f32[128,128]{1,0:T(8,128)S(1)}, f32[128,128]{1,0:T(8,128)}, u32[]{:S(2)}) copy-start(f32[128,128]{1,0:T(8,128)} %bd_ref.1) | copy-start | bytes 196612
  0.7 75.0 %copy-start.4 = (f32[1024]{0:T(1024)S(1)}, f32[1024]{0:T(1024)}, u32[]{:S(2)}) copy-start(f32[1024]{0:T(1024)} %param.14) | copy-start | bytes 12292
  7.7 67.9 %copy-start.1 = (f32[1024,1024]{1,0:T(8,128)S(1)}, f32[1024,1024]{1,0:T(8,128)}, u32[]{:S(2)}) copy-start(f32[1024,1024]{1,0:T(8,128)} %bx_ref.1) | copy-start | bytes 12582916
  7.7 67.9 %copy-start.3 = (f32[1024]{0:T(1024)S(1)}, f32[1024]{0:T(1024)}, u32[]{:S(2)}) copy-start(f32[1024]{0:T(1024)} %param.13) | copy-start | bytes 12292
  7.7 67.9 %copy-start.5 = (f32[128]{0:T(128)S(1)}, f32[128]{0:T(128)}, u32[]{:S(2)}) copy-start(f32[128]{0:T(128)} %param.12) | copy-start | bytes 1540
  84.9 59.6 %copy-start = (f32[1024,1024]{1,0:T(8,128)S(1)}, f32[1024,1024]{1,0:T(8,128)}, u32[]{:S(2)}) copy-start(f32[1024,1024]{1,0:T(8,128)} %by_ref.3) | copy-start | bytes 12582916

commit v3 on v2

--- a/solution.py
+++ b/solution.py
@@ -13,6 +13,7 @@
 ORDER = ("zh", "zl", "core", "x", "y")
 NB = 2
 ROWS = NB * 256
+PIECES = 2
 WIDE = 16
 
 
@@ -45,14 +46,46 @@
     return w0, w1, w2, w3
 
 
-def forward_y(_, f_ref, by_ref, out_ref, cols):
-    cols[...] = dot3(split(by_ref[...]), split(f_ref[...]), ((0,), (1,)))
-    out = out_ref.reshape(256 * 4 * NB, 128)
-    for bl in range(NB):
-        for q in range(4):
-            out[pl.ds(bl * 4 + q, 256, stride=4 * NB), :] = cols[
-                pl.ds(bl * 256, 256), pl.ds(q * 128, 128)
-            ]
+def forward_y(_, f_hbm, by_hbm, out_ref, field, by, high, low, sems):
+    step = f_hbm.shape[1] // PIECES
+    pieces = [pl.ds(i * step, step) for i in range(PIECES)]
+
+    def load_field(i):
+        return pltpu.make_async_copy(f_hbm.at[:, pieces[i]], field.at[:, pieces[i]], sems.at[0, i])
+
+    def load_by(half, i):
+        return pltpu.make_async_copy(
+            by_hbm.at[pieces[i], pl.ds(half * ROWS, ROWS)], by.at[half, pieces[i], :], sems.at[1 + half, i]
+        )
+
+    def work(half):
+        cols = None
+        for i, piece in enumerate(pieces):
+            if half == 0:
+                load_field(i).wait()
+                high[:, piece], low[:, piece] = split(field[:, piece])
+            load_by(half, i).wait()
+            part = dot3(split(by[half, piece, :]), (high[:, piece], low[:, piece]), ((0,), (1,)))
+            cols = part if cols is None else cols + part
+        out = out_ref.reshape(256 * 4 * NB, 128)
+        for bl in range(NB):
+            for q in range(4):
+                out[pl.ds(bl * 4 + q, 256, stride=4 * NB), :] = cols[
+                    bl * 256 : (bl + 1) * 256, q * 128 : (q + 1) * 128
+                ]
+
+    @pl.when(pl.program_id(0) == 0)
+    def _():
+        for i in range(PIECES):
+            load_field(i).start()
+            load_by(0, i).start()
+        for i in range(PIECES):
+            load_by(1, i).start()
+        work(0)
+
+    @pl.when(pl.program_id(0) == 1)
+    def _():
+        work(1)
 
 
 def row_index(shape, dim):
@@ -147,11 +180,17 @@
         grid=(cols // ROWS,),
         in_specs=[
             pl.BlockSpec(memory_space=pltpu.SMEM),
-            pl.BlockSpec(flat.shape, lambda c: (0, 0)),
-            pl.BlockSpec((cols, ROWS), lambda c: (0, c)),
+            pl.BlockSpec(memory_space=pl.ANY),
+            pl.BlockSpec(memory_space=pl.ANY),
         ],
         out_specs=pl.BlockSpec((256, 4 * NB, 128), lambda c: (0, c, 0)),
-        scratch_shapes=[pltpu.VMEM((ROWS, days * rows), F32)],
+        scratch_shapes=[
+            pltpu.VMEM(flat.shape, F32),
+            pltpu.VMEM((2, cols, ROWS), F32),
+            pltpu.VMEM(flat.shape, BF16),
+            pltpu.VMEM(flat.shape, BF16),
+            pltpu.SemaphoreType.DMA((3, PIECES)),
+        ],
         compiler_params=limit(60),
         name="forward_y",
     )(noise, flat, basis_y)

time: 150 us -> 150 us (level)
  no operation moved by 1% of the time
where the time goes in v3:
time: 150 us
  blocking collectives  127 us (85%)
  Pallas kernels  21.4 us (14%)
    all_to_all x2, blocking collectives, exchange(): lax.all_to_all(parts, ORDER, 0, 0, tiled=True).reshape(256 * WIDE, 128)  127 us
    pallas_call x1, Pallas kernels, body(): pl.pallas_call(middle, out_shape=jax.ShapeDtypeStruct((256 * WIDE, 128),...  9.27 us
    pallas_call x1, Pallas kernels, body(): pl.pallas_call(forward_y, out_shape=jax.ShapeDtypeStruct((256, WIDE, 128)...  6.72 us
    pallas_call x1, Pallas kernels, body(): pl.pallas_call(inverse_y, out_shape=jax.ShapeDtypeStruct(flat.shape, F32)...  5.39 us

profile of v3, /device:TPU:1, one launch (start us, length us, event | category | flops | bytes accessed | tf_op | source)
XLA Modules:
  0.0 149.6 jit_solution(614219070323578414)
XLA Ops:
  0.7 0.0 copy-start.2
  0.7 0.0 copy-start.4
  0.7 6.7 %forward_y.1 = f32[256,16,128]{2,1,0:T(8,128)} custom-call(f32[1]{0:T(128)S(6)} %copy.9._.noise_ref, f32[512,1024]{1,0:T(8,128)} %bitcast.14, f32[1024,1024]{1,0:T(8,128)} %by_ref.1), custom_call_target="tpu_custom_call" | custom-call | tf_op jit(solution)/shard_map/forward_y/pallas_call | solution.py:177
  7.4 0.0 copy-start.1
  7.4 0.0 copy-start.3
  7.4 0.0 copy-start.5
  7.4 67.9 %all_to_all.10 = f32[256,16,128]{2,1,0:T(8,128)S(1)} all-to-all(f32[256,16,128]{2,1,0:T(8,128)} %forward_y.1), channel_id=1, replica_groups=mesh['zh'=4,'core'=2,'zl'=2,'x'=4,'y'=4] {'zh','zl','core','x','y'}, dimensions={0} | all-to-all | bytes 4194304 | tf_op jit(solution)/shard_map/all_to_all | solution.py:171
  75.3 0.0 copy-done.2
  75.3 0.0 copy-done.4
  75.3 0.0 copy-done.1
  75.4 0.0 copy-done.3
  75.4 0.0 copy-done.5
  75.4 9.3 %middle.1 = f32[4096,128]{1,0:T(8,128)S(1)} custom-call(f32[4096,128]{1,0:T(8,128)S(1)} %bitcast.8, f32[1024,1024]{1,0:T(8,128)S(1)} %copy-done.1, f32[128,128]{1,0:T(8,128)S(1)} %copy-done.2, f32[1,128]{1,0:T(1,128)S(1)} %bitcast.13, f32[1,1024]{1,0:T(1,128)S(1)} %bitcast.11, f32[1,1024]{1,0:T(1,128)S(1)} %bitcast.12, f32[1]{0:T(128)S(6)} %copy.9._.noise_ref), custom_call_target="tpu_custom_call" | custom-call | tf_op jit(solution)/shard_map/middle/pallas_call | solution.py:197
  84.6 0.0 copy-start
  84.7 59.6 %all_to_all.11 = f32[256,16,128]{2,1,0:T(8,128)S(1)} all-to-all(f32[256,16,128]{2,1,0:T(8,128)S(1)} %bitcast.9), channel_id=1, replica_groups=mesh['zh'=4,'core'=2,'zl'=2,'x'=4,'y'=4] {'zh','zl','core','x','y'}, dimensions={0} | all-to-all | bytes 4194304 | tf_op jit(solution)/shard_map/all_to_all | solution.py:171
  144.2 0.0 copy-done
  144.2 5.4 %inverse_y.1 = f32[512,1024]{1,0:T(8,128)} custom-call(f32[4096,128]{1,0:T(8,128)S(1)} %bitcast.10, f32[1024,1024]{1,0:T(8,128)S(1)} %copy-done), custom_call_target="tpu_custom_call" | custom-call | tf_op jit(solution)/shard_map/inverse_y/pallas_call | solution.py:214
Async XLA Ops:
  0.7 74.7 %copy-start.2 = (f32[128,128]{1,0:T(8,128)S(1)}, f32[128,128]{1,0:T(8,128)}, u32[]{:S(2)}) copy-start(f32[128,128]{1,0:T(8,128)} %bd_ref.1) | copy-start | bytes 196612
  0.7 74.7 %copy-start.4 = (f32[1024]{0:T(1024)S(1)}, f32[1024]{0:T(1024)}, u32[]{:S(2)}) copy-start(f32[1024]{0:T(1024)} %param.14) | copy-start | bytes 12292
  7.4 68.0 %copy-start.1 = (f32[1024,1024]{1,0:T(8,128)S(1)}, f32[1024,1024]{1,0:T(8,128)}, u32[]{:S(2)}) copy-start(f32[1024,1024]{1,0:T(8,128)} %bx_ref.1) | copy-start | bytes 12582916
  7.4 67.9 %copy-start.3 = (f32[1024]{0:T(1024)S(1)}, f32[1024]{0:T(1024)}, u32[]{:S(2)}) copy-start(f32[1024]{0:T(1024)} %param.13) | copy-start | bytes 12292
  7.4 67.9 %copy-start.5 = (f32[128]{0:T(128)S(1)}, f32[128]{0:T(128)}, u32[]{:S(2)}) copy-start(f32[128]{0:T(128)} %param.12) | copy-start | bytes 1540
  84.6 59.6 %copy-start = (f32[1024,1024]{1,0:T(8,128)S(1)}, f32[1024,1024]{1,0:T(8,128)}, u32[]{:S(2)}) copy-start(f32[1024,1024]{1,0:T(8,128)} %by_ref.1) | copy-start | bytes 12582916

commit v4 on v3

--- a/solution.py
+++ b/solution.py
@@ -27,6 +27,12 @@
         lax.dot_general, dimension_numbers=(dims, ((), ())), preferred_element_type=F32
     )
     return mul(a[0], b[0]) + (mul(a[0], b[1]) + mul(a[1], b[0]))
+
+
+def dot3_long(a, b, dims=((1,), (0,))):
+    left = jnp.concatenate([a[0], a[0], a[1]], dims[0][0])
+    right = jnp.concatenate([b[0], b[1], b[0]], dims[1][0])
+    return lax.dot_general(left, right, (dims, ((), ())), preferred_element_type=F32)
 
 
 def swap_groups(v):
@@ -137,10 +143,10 @@
         for i in range(NB):
             own = jnp.where(column == half * ROWS + i * 256 + mine, ey_ref[...], 0.0)
             ey = jnp.where(bl[:, :1] == i, jnp.sum(own, 1, keepdims=True), ey)
-        along_x = dot3(split(work[...]), bx)
-        spectral = dot3(to_s, split(along_x))
-        back_day = dot3(to_t, split(spectral / (edx * ey + noise_ref[0])))
-        work[...] = dot3(split(back_day), bx, ((1,), (1,)))
+        along_x = dot3_long(split(work[...]), bx)
+        spectral = dot3_long(to_s, split(along_x))
+        back_day = dot3_long(to_t, split(spectral / (edx * ey + noise_ref[0])))
+        work[...] = dot3_long(split(back_day), bx, ((1,), (1,)))
         for ys, tls, lanes in blocks(half):
             for rows, part in zip(ys, swap_groups([work[t, lanes] for t in tls])):
                 out_ref[rows, :] = part

time: 150 us -> 150 us (level)
  no operation moved by 1% of the time
where the time goes in v4:
time: 150 us; the launch traced here: 149 us
  blocking collectives  127 us (85%)
  Pallas kernels  21.2 us (14%)
    all_to_all x2, blocking collectives, exchange(): lax.all_to_all(parts, ORDER, 0, 0, tiled=True).reshape(256 * WIDE, 128)  127 us
    pallas_call x1, Pallas kernels, body(): pl.pallas_call(middle, out_shape=jax.ShapeDtypeStruct((256 * WIDE, 128),...  9.06 us
    pallas_call x1, Pallas kernels, body(): pl.pallas_call(forward_y, out_shape=jax.ShapeDtypeStruct((256, WIDE, 128)...  6.72 us
    pallas_call x1, Pallas kernels, body(): pl.pallas_call(inverse_y, out_shape=jax.ShapeDtypeStruct(flat.shape, F32)...  5.39 us

profile of v4, /device:TPU:1, one launch (start us, length us, event | category | flops | bytes accessed | tf_op | source)
XLA Modules:
  0.0 149.4 jit_solution(8532189959178340168)
XLA Ops:
  0.7 0.0 copy-start.2
  0.7 0.0 copy-start.4
  0.7 6.7 %forward_y.1 = f32[256,16,128]{2,1,0:T(8,128)} custom-call(f32[1]{0:T(128)S(6)} %copy.9._.noise_ref, f32[512,1024]{1,0:T(8,128)} %bitcast.14, f32[1024,1024]{1,0:T(8,128)} %by_ref.1), custom_call_target="tpu_custom_call" | custom-call | tf_op jit(solution)/shard_map/forward_y/pallas_call | solution.py:183
  7.4 0.0 copy-start.1
  7.4 0.0 copy-start.3
  7.4 0.0 copy-start.5
  7.4 67.9 %all_to_all.10 = f32[256,16,128]{2,1,0:T(8,128)S(1)} all-to-all(f32[256,16,128]{2,1,0:T(8,128)} %forward_y.1), channel_id=1, replica_groups=mesh['zh'=4,'core'=2,'zl'=2,'x'=4,'y'=4] {'zh','zl','core','x','y'}, dimensions={0} | all-to-all | bytes 4194304 | tf_op jit(solution)/shard_map/all_to_all | solution.py:177
  75.3 0.0 copy-done.2
  75.3 0.0 copy-done.4
  75.3 0.0 copy-done.1
  75.4 0.0 copy-done.3
  75.4 0.0 copy-done.5
  75.4 9.1 %middle.1 = f32[4096,128]{1,0:T(8,128)S(1)} custom-call(f32[4096,128]{1,0:T(8,128)S(1)} %bitcast.8, f32[1024,1024]{1,0:T(8,128)S(1)} %copy-done.1, f32[128,128]{1,0:T(8,128)S(1)} %copy-done.2, f32[1,128]{1,0:T(1,128)S(1)} %bitcast.13, f32[1,1024]{1,0:T(1,128)S(1)} %bitcast.11, f32[1,1024]{1,0:T(1,128)S(1)} %bitcast.12, f32[1]{0:T(128)S(6)} %copy.9._.noise_ref), custom_call_target="tpu_custom_call" | custom-call | tf_op jit(solution)/shard_map/middle/pallas_call | solution.py:203
  84.4 0.0 copy-start
  84.4 59.6 %all_to_all.11 = f32[256,16,128]{2,1,0:T(8,128)S(1)} all-to-all(f32[256,16,128]{2,1,0:T(8,128)S(1)} %bitcast.9), channel_id=1, replica_groups=mesh['zh'=4,'core'=2,'zl'=2,'x'=4,'y'=4] {'zh','zl','core','x','y'}, dimensions={0} | all-to-all | bytes 4194304 | tf_op jit(solution)/shard_map/all_to_all | solution.py:177
  144.0 0.0 copy-done
  144.0 5.4 %inverse_y.1 = f32[512,1024]{1,0:T(8,128)} custom-call(f32[4096,128]{1,0:T(8,128)S(1)} %bitcast.10, f32[1024,1024]{1,0:T(8,128)S(1)} %copy-done), custom_call_target="tpu_custom_call" | custom-call | tf_op jit(solution)/shard_map/inverse_y/pallas_call | solution.py:220
Async XLA Ops:
  0.7 74.7 %copy-start.2 = (f32[128,128]{1,0:T(8,128)S(1)}, f32[128,128]{1,0:T(8,128)}, u32[]{:S(2)}) copy-start(f32[128,128]{1,0:T(8,128)} %bd_ref.1) | copy-start | bytes 196612
  0.7 74.7 %copy-start.4 = (f32[1024]{0:T(1024)S(1)}, f32[1024]{0:T(1024)}, u32[]{:S(2)}) copy-start(f32[1024]{0:T(1024)} %param.14) | copy-start | bytes 12292
  7.4 68.0 %copy-start.1 = (f32[1024,1024]{1,0:T(8,128)S(1)}, f32[1024,1024]{1,0:T(8,128)}, u32[]{:S(2)}) copy-start(f32[1024,1024]{1,0:T(8,128)} %bx_ref.1) | copy-start | bytes 12582916
  7.4 67.9 %copy-start.3 = (f32[1024]{0:T(1024)S(1)}, f32[1024]{0:T(1024)}, u32[]{:S(2)}) copy-start(f32[1024]{0:T(1024)} %param.13) | copy-start | bytes 12292
  7.4 67.9 %copy-start.5 = (f32[128]{0:T(128)S(1)}, f32[128]{0:T(128)}, u32[]{:S(2)}) copy-start(f32[128]{0:T(128)} %param.12) | copy-start | bytes 1540
  84.4 59.6 %copy-start = (f32[1024,1024]{1,0:T(8,128)S(1)}, f32[1024,1024]{1,0:T(8,128)}, u32[]{:S(2)}) copy-start(f32[1024,1024]{1,0:T(8,128)} %by_ref.1) | copy-start | bytes 12582916

commit v5 on v4

--- a/solution.py
+++ b/solution.py
@@ -152,7 +152,7 @@
                 out_ref[rows, :] = part
 
 
-def inverse_y(r_ref, by_ref, out_ref, cols, high, low):
+def inverse_y(r_ref, by_ref, out_ref, cols, left):
     @pl.when(pl.program_id(0) == 0)
     def _():
         for bl in range(WIDE // 4):
@@ -160,9 +160,13 @@
                 cols[pl.ds(bl * 256, 256), pl.ds(q * 128, 128)] = r_ref[
                     pl.ds(bl * 4 + q, 256, stride=WIDE), :
                 ]
-        high[...], low[...] = split(cols[...].T)
-
-    out_ref[...] = dot3((high[...], low[...]), split(by_ref[...]), ((1,), (1,)))
+        high, low = split(cols[...].T)
+        n = high.shape[1]
+        left[:, :n], left[:, n : 2 * n], left[:, 2 * n :] = high, high, low
+
+    high, low = split(by_ref[...])
+    right = jnp.concatenate([high, low, high], 1)
+    out_ref[...] = lax.dot_general(left[...], right, (((1,), (1,)), ((), ())), preferred_element_type=F32)
 
 
 VMEM = pl.BlockSpec(memory_space=pltpu.VMEM)
@@ -228,8 +232,7 @@
         out_specs=pl.BlockSpec((days * rows, cols // 2), lambda c: (0, c)),
         scratch_shapes=[
             pltpu.VMEM((cols, days * rows), F32),
-            pltpu.VMEM((days * rows, cols), BF16),
-            pltpu.VMEM((days * rows, cols), BF16),
+            pltpu.VMEM((days * rows, 3 * cols), BF16),
         ],
         compiler_params=limit(40),
         name="inverse_y",

time: 150 us -> 150 us (level)
  no operation moved by 1% of the time
where the time goes in v5:
time: 150 us
  blocking collectives  127 us (85%)
  Pallas kernels  21.3 us (14%)
    all_to_all x2, blocking collectives, exchange(): lax.all_to_all(parts, ORDER, 0, 0, tiled=True).reshape(256 * WIDE, 128)  127 us
    pallas_call x1, Pallas kernels, body(): pl.pallas_call(middle, out_shape=jax.ShapeDtypeStruct((256 * WIDE, 128),...  9.06 us
    pallas_call x1, Pallas kernels, body(): pl.pallas_call(forward_y, out_shape=jax.ShapeDtypeStruct((256, WIDE, 128)...  6.72 us
    pallas_call x1, Pallas kernels, body(): pl.pallas_call(inverse_y, out_shape=jax.ShapeDtypeStruct(flat.shape, F32)...  5.5 us

profile of v5, /device:TPU:1, one launch (start us, length us, event | category | flops | bytes accessed | tf_op | source)
XLA Modules:
  0.0 149.5 jit_solution(7593899781966055507)
XLA Ops:
  0.7 0.0 copy-start.2
  0.7 0.0 copy-start.4
  0.7 6.7 %forward_y.1 = f32[256,16,128]{2,1,0:T(8,128)} custom-call(f32[1]{0:T(128)S(6)} %copy.9._.noise_ref, f32[512,1024]{1,0:T(8,128)} %bitcast.14, f32[1024,1024]{1,0:T(8,128)} %by_ref.1), custom_call_target="tpu_custom_call" | custom-call | tf_op jit(solution)/shard_map/forward_y/pallas_call | solution.py:187
  7.4 0.0 copy-start.1
  7.4 0.0 copy-start.3
  7.4 0.0 copy-start.5
  7.4 67.9 %all_to_all.10 = f32[256,16,128]{2,1,0:T(8,128)S(1)} all-to-all(f32[256,16,128]{2,1,0:T(8,128)} %forward_y.1), channel_id=1, replica_groups=mesh['zh'=4,'core'=2,'zl'=2,'x'=4,'y'=4] {'zh','zl','core','x','y'}, dimensions={0} | all-to-all | bytes 4194304 | tf_op jit(solution)/shard_map/all_to_all | solution.py:181
  75.3 0.0 copy-done.2
  75.3 0.0 copy-done.4
  75.3 0.0 copy-done.1
  75.4 0.0 copy-done.3
  75.4 0.0 copy-done.5
  75.4 9.1 %middle.1 = f32[4096,128]{1,0:T(8,128)S(1)} custom-call(f32[4096,128]{1,0:T(8,128)S(1)} %bitcast.8, f32[1024,1024]{1,0:T(8,128)S(1)} %copy-done.1, f32[128,128]{1,0:T(8,128)S(1)} %copy-done.2, f32[1,128]{1,0:T(1,128)S(1)} %bitcast.13, f32[1,1024]{1,0:T(1,128)S(1)} %bitcast.11, f32[1,1024]{1,0:T(1,128)S(1)} %bitcast.12, f32[1]{0:T(128)S(6)} %copy.9._.noise_ref), custom_call_target="tpu_custom_call" | custom-call | tf_op jit(solution)/shard_map/middle/pallas_call | solution.py:207
  84.4 0.0 copy-start
  84.4 59.6 %all_to_all.11 = f32[256,16,128]{2,1,0:T(8,128)S(1)} all-to-all(f32[256,16,128]{2,1,0:T(8,128)S(1)} %bitcast.9), channel_id=1, replica_groups=mesh['zh'=4,'core'=2,'zl'=2,'x'=4,'y'=4] {'zh','zl','core','x','y'}, dimensions={0} | all-to-all | bytes 4194304 | tf_op jit(solution)/shard_map/all_to_all | solution.py:181
  144.0 0.0 copy-done
  144.0 5.5 %inverse_y.1 = f32[512,1024]{1,0:T(8,128)} custom-call(f32[4096,128]{1,0:T(8,128)S(1)} %bitcast.10, f32[1024,1024]{1,0:T(8,128)S(1)} %copy-done), custom_call_target="tpu_custom_call" | custom-call | tf_op jit(solution)/shard_map/inverse_y/pallas_call | solution.py:224
Async XLA Ops:
  0.7 74.7 %copy-start.2 = (f32[128,128]{1,0:T(8,128)S(1)}, f32[128,128]{1,0:T(8,128)}, u32[]{:S(2)}) copy-start(f32[128,128]{1,0:T(8,128)} %bd_ref.1) | copy-start | bytes 196612
  0.7 74.7 %copy-start.4 = (f32[1024]{0:T(1024)S(1)}, f32[1024]{0:T(1024)}, u32[]{:S(2)}) copy-start(f32[1024]{0:T(1024)} %param.14) | copy-start | bytes 12292
  7.4 68.0 %copy-start.1 = (f32[1024,1024]{1,0:T(8,128)S(1)}, f32[1024,1024]{1,0:T(8,128)}, u32[]{:S(2)}) copy-start(f32[1024,1024]{1,0:T(8,128)} %bx_ref.1) | copy-start | bytes 12582916
  7.4 67.9 %copy-start.3 = (f32[1024]{0:T(1024)S(1)}, f32[1024]{0:T(1024)}, u32[]{:S(2)}) copy-start(f32[1024]{0:T(1024)} %param.13) | copy-start | bytes 12292
  7.4 67.9 %copy-start.5 = (f32[128]{0:T(128)S(1)}, f32[128]{0:T(128)}, u32[]{:S(2)}) copy-start(f32[128]{0:T(128)} %param.12) | copy-start | bytes 1540
  84.4 59.6 %copy-start = (f32[1024,1024]{1,0:T(8,128)S(1)}, f32[1024,1024]{1,0:T(8,128)}, u32[]{:S(2)}) copy-start(f32[1024,1024]{1,0:T(8,128)} %by_ref.1) | copy-start | bytes 12582916
